TPU v7x, 32 devices: a whole 2x2x4 slice. The times are simulated.
32 devices in a mesh: tm: 8 (over y, x, core), floor: 4 (over z).
Axes of the slice: x: 2, y: 2, z: 4, core: 2. Of those that a mesh axis runs over, the one named last changes fastest.
Arguments:
- samples: bfloat16 [8, 16, 32768], P('tm', None, 'floor'), may hold values from -6 to 6
- operator: bfloat16 [8, 512, 32768], P('tm', None, 'floor'), may hold values from -0.01171875 to 0.01171875
Outputs:
- sensor_data: bfloat16 [8, 16, 512], P('tm', None, 'floor')
All inputs are finite; a program needn't handle non-finite values.
Results may differ from a plain program's by a relative error of at most 0.0013.
Values may be sent and summed in bfloat16 or wider, within the bound.
A program may use at most 64 MiB of HBM per device.

v0:
```python
import functools

import jax
import jax.numpy as jnp
from jax import lax
from jax.experimental import pallas as pl
from jax.experimental.pallas import tpu as pltpu
from jax.sharding import PartitionSpec as P

MESH = pl.DeviceIdType.MESH
LOOK = 1


def each(low, high, body):
    if high - low <= 4:
        for i in range(low, high):
            body(i)
    else:
        def step(i, carry):
            body(i)
            return carry

        lax.fori_loop(low, high, step, 0)


def grid_of(chips):
    rows = 1
    while rows * rows * 4 <= chips and chips % (rows * 2) == 0:
        rows *= 2
    return rows, chips // rows


def kernel(
    n, m, chunks, x_hbm, op_hbm, out_ref, x, far, op, acc, part, total, share,
    own_sem, op_sem, out_sem, pair_sem, fwd_sem, relay_sem, in_sem,
    red_out, red_in, floor_out, floor_in,
):
    me, floor = lax.axis_index("tm"), lax.axis_index("floor")
    chips = n // 2
    rows, cols = grid_of(chips)
    chip, core = lax.div(me, 2), lax.rem(me, 2)
    row, col = lax.div(chip, cols), lax.rem(chip, cols)
    pair = 2 * chip + 1 - core
    k, width = x.shape[2], x.shape[3]
    sensors = op.shape[1]
    share_size = sensors // m

    def columns(c):
        return pl.ds(c * width, width)

    own = [pltpu.make_async_copy(x_hbm.at[0, :, columns(c)], x.at[c, me], own_sem.at[c]) for c in range(chunks)]
    weights = [pltpu.make_async_copy(op_hbm.at[0, :, columns(c)], op.at[c], op_sem.at[c]) for c in range(chunks)]
    for c in range(chunks):
        own[c].start()
        weights[c].start()

    barrier = pltpu.get_barrier_semaphore()
    for step in range(1, n):
        pl.semaphore_signal(barrier, inc=1, device_id={"tm": lax.rem(me + step, n)}, device_id_type=MESH)
    for step in range(1, m):
        pl.semaphore_signal(barrier, inc=1, device_id={"floor": lax.rem(floor + step, m)}, device_id_type=MESH)
    pl.semaphore_wait(barrier, n + m - 2)

    def need(block, at_chip):
        return 2 * at_chip + block < n

    many = max(rows, cols)

    def straight(source, at):
        return (lax.div(source, cols) == lax.div(at, cols)) | (lax.rem(source, cols) == lax.rem(at, cols))

    def relayed(odd, source, block, at, step):
        turn = lax.rem(core + odd, 2) == 0
        r, q = lax.div(source, cols), lax.rem(source, cols)
        r_at, q_at = lax.div(at, cols), lax.rem(at, cols)
        r_to, q_to = lax.rem(r + step, rows), lax.rem(q + step, cols)
        down = (r_at == r) & (step < rows) & (turn | ((r_to == 0) & (q == 0)))
        along = (q_at == q) & (step < cols) & (jnp.logical_not(turn) | ((q_to == 0) & (r == 0)))
        target = jnp.where(r_at == r, r_to * cols + q_at, r_at * cols + q_to)
        return (at != 0) & (down | along) & need(block, target), 2 * target + core

    def route(odd, source, block, at):
        passes = at < 0
        for step in range(1, many):
            passes = passes | relayed(odd, source, block, at, step)[0]
        return straight(source, at) & (need(block, at) | passes), passes

    def make_plan(step, odd):
        other = lax.rem(chip + step, chips)
        block = 2 * other + core
        wanted, _ = route(odd, chip, me, other)
        _, passes = route(odd, other, block, chip)
        near = straight(other, chip)
        here = need(block, chip) & near, need(block, chip) & jnp.logical_not(near)
        alone = here[0] & jnp.logical_not(passes)
        onward = [relayed(odd, other, block, chip, s) for s in range(1, many)]
        return other, block, wanted, passes, here, alone, onward

    plans = {}
    if chips <= 5:
        plans = {(step, odd): make_plan(step, odd) for step in range(1, chips) for odd in (0, 1)}

    def plan(step, c):
        return plans[step, c % 2] if plans else make_plan(step, c % 2)

    others = [2 * lax.rem(chip + step, chips) + 1 - core for step in range(chips)] if plans else None
    def other_here(block):
        near = straight(lax.div(block, 2), chip)
        return need(block, chip) & near, need(block, chip) & jnp.logical_not(near)

    others_here = [other_here(block) for block in others] if plans else None
    self_here = need(me, chip)

    busy = need(2 * row * cols, chip) | need(2 * col, chip)

    def send(c, block, target, sem, source=None, into=None):
        return pltpu.make_async_remote_copy(
            src_ref=x.at[c, block] if source is None else source,
            dst_ref=(x if into is None else into).at[c, block],
            send_sem=sem, recv_sem=in_sem.at[c, block], device_id={"tm": target}, device_id_type=MESH,
        )

    def mine(c):
        return x_hbm.at[0, :, columns(c)]

    def sends(c, act):
        def one(step):
            _, block, wanted, *_ = plan(step, c)

            @pl.when(wanted)
            def _():
                act(send(c, me, block, out_sem.at[c, step], mine(c)))

        each(1, chips, one)

        @pl.when(self_here)
        def _():
            act(send(c, me, pair, pair_sem.at[c], mine(c)))

    def relays(c, act, wait):
        def one(step):
            source, block, _, passes, _, _, onward = plan(step, c)

            @pl.when(passes)
            def _():
                if wait:
                    send(c, block, pair, fwd_sem.at[c, source]).wait_recv()
                for s, (wanted, target) in enumerate(onward):
                    @pl.when(wanted)
                    def _(s=s, target=target):
                        act(send(c, block, target, relay_sem.at[c, source, s], None, far))

        each(1, chips, one)

    def forwards(c, act, wait):
        def one(step):
            source, block, _, _, here, alone, _ = plan(step, c)
            if wait:
                @pl.when(alone)
                def _():
                    send(c, block, pair, fwd_sem.at[c, source]).wait_recv()

            @pl.when(here[0])
            def _():
                act(send(c, block, pair, fwd_sem.at[c, source]))

        each(1, chips, one)

    def far_forwards(c, act, wait):
        def one(step):
            source, block, _, _, here, _, _ = plan(step, c)

            @pl.when(here[1])
            def _():
                copy = send(c, block, pair, fwd_sem.at[c, source], far.at[c, block], far)
                if wait:
                    copy.wait_recv()
                act(copy)

        each(1, chips, one)

    def take(c, part_of):
        def one(step):
            block = others[step] if plans else 2 * lax.rem(chip + step, chips) + 1 - core
            here = (others_here[step] if plans else other_here(block))[part_of]

            @pl.when(here)
            def _():
                send(c, block, pair, pair_sem.at[c], None, far if part_of else None).wait_recv()

        each(0, chips, one)

    def start(copy):
        copy.start()

    def wait_send(copy):
        copy.wait_send()


    tile = min(n, max(1, 128 // k))

    def image_of(block_rows, c):
        return lax.dot_general(
            block_rows.reshape(-1, width), op[c], (((1,), (1,)), ((), ())), preferred_element_type=jnp.float32
        ).reshape(-1, k, sensors)

    for c in range(chunks):
        sends(c, start)
    for c in range(min(LOOK, chunks)):
        relays(c, start, True)
    forwards(0, start, True)
    for c in range(chunks):
        if c + LOOK < chunks:
            relays(c + LOOK, start, True)
        if c + 1 < chunks:
            forwards(c + 1, start, True)
        take(c, 0)
        own[c].wait()
        weights[c].wait()

        @pl.when(busy)
        def _(c=c):
            for r in range(n // tile):
                image = image_of(x[c, r * tile:(r + 1) * tile], c)
                if c == 0:
                    acc[r * tile:(r + 1) * tile] = image
                else:
                    acc[r * tile:(r + 1) * tile] += image

    def lag_part(step):
        return pltpu.make_async_remote_copy(
            src_ref=acc.at[step], dst_ref=part.at[me],
            send_sem=red_out.at[step], recv_sem=red_in.at[me],
            device_id={"tm": lax.rem(me + step, n)}, device_id_type=MESH,
        )

    def lag_parts(near, act):
        for step in range(n - 1, 0, -1):
            @pl.when((me + step < n) & (straight(step // 2, chip) == near))
            def _(step=step):
                act(lag_part(step))

    lag_parts(True, start)

    far_forwards(0, start, True)
    for c in range(chunks):
        if c + 1 < chunks:
            far_forwards(c + 1, start, True)
        take(c, 1)

        def far_images(step, c=c):
            r = lax.rem(row + 1 + lax.div(step, max(1, cols - 1)), rows)
            q = lax.rem(col + 1 + lax.rem(step, max(1, cols - 1)), cols)
            source = r * cols + q

            @pl.when(need(2 * source, chip))
            def _():
                image = image_of(far[c, pl.ds(2 * source, 2)], c)
                if c == 0:
                    acc[pl.ds(2 * source, 2)] = image
                else:
                    acc[pl.ds(2 * source, 2)] += image

        each(0, (rows - 1) * (cols - 1), far_images)

    lag_parts(False, start)

    for c in range(chunks):
        sends(c, wait_send)
        relays(c, wait_send, False)
        forwards(c, wait_send, False)
        far_forwards(c, wait_send, False)

    def add_lag(lag, value):
        pltpu.make_async_remote_copy(
            src_ref=acc.at[0], dst_ref=part.at[lag],
            send_sem=red_out.at[0], recv_sem=red_in.at[lag],
            device_id={"tm": pair}, device_id_type=MESH,
        ).wait_recv()
        return value + part[lag]

    value = lax.fori_loop(0, me, add_lag, acc[0])
    for j in range(m):
        total[j] = value[:, j * share_size:(j + 1) * share_size]

    def to_floor(step):
        other = lax.rem(floor + step, m)
        return pltpu.make_async_remote_copy(
            src_ref=total.at[other], dst_ref=share.at[floor],
            send_sem=floor_out.at[step], recv_sem=floor_in.at[floor],
            device_id={"floor": other}, device_id_type=MESH,
        )

    for step in range(m - 1, 0, -1):
        to_floor(step).start()
    result = total[floor]
    for step in range(1, m):
        source = lax.rem(floor + step, m)
        pltpu.make_async_remote_copy(
            src_ref=total.at[source], dst_ref=share.at[source],
            send_sem=floor_out.at[step], recv_sem=floor_in.at[source],
            device_id={"floor": source}, device_id_type=MESH,
        ).wait_recv()
        result = result + share[source]
    out_ref[0] = result.astype(out_ref.dtype)

    lag_parts(True, wait_send)
    lag_parts(False, wait_send)
    for step in range(1, m):
        to_floor(step).wait_send()


def solution(mesh):
    n, m = mesh.shape["tm"], mesh.shape["floor"]

    def local(samples, operator):
        _, k, depth = samples.shape
        sensors = operator.shape[1]
        chunks = 4
        width = depth // chunks
        return pl.pallas_call(
            functools.partial(kernel, n, m, chunks),
            out_shape=jax.ShapeDtypeStruct((1, k, sensors // m), jnp.bfloat16),
            in_specs=[pl.BlockSpec(memory_space=pl.ANY)] * 2,
            out_specs=pl.BlockSpec(memory_space=pltpu.VMEM),
            scratch_shapes=[
                pltpu.VMEM((chunks, n, k, width), jnp.bfloat16),
                pltpu.VMEM((chunks, n, k, width), jnp.bfloat16),
                pltpu.VMEM((chunks, sensors, width), jnp.bfloat16),
                pltpu.VMEM((n, k, sensors), jnp.float32),
                pltpu.VMEM((n, k, sensors), jnp.float32),
                pltpu.VMEM((m, k, sensors // m), jnp.float32),
                pltpu.VMEM((m, k, sensors // m), jnp.float32),
                pltpu.SemaphoreType.DMA((chunks,)),
                pltpu.SemaphoreType.DMA((chunks,)),
                pltpu.SemaphoreType.DMA((chunks, n // 2)),
                pltpu.SemaphoreType.DMA((chunks,)),
                pltpu.SemaphoreType.DMA((chunks, n // 2)),
                pltpu.SemaphoreType.DMA((chunks, n // 2, max(1, max(grid_of(n // 2)) - 1))),
                pltpu.SemaphoreType.DMA((chunks, n)),
                pltpu.SemaphoreType.DMA((n,)),
                pltpu.SemaphoreType.DMA((n,)),
                pltpu.SemaphoreType.DMA((m,)),
                pltpu.SemaphoreType.DMA((m,)),
            ],
            compiler_params=pltpu.CompilerParams(collective_id=0, has_side_effects=True),
        )(samples, operator)

    placed = (P("tm", None, "floor"), P("tm", None, "floor"))
    return jax.shard_map(
        local, mesh=mesh, in_specs=placed, out_specs=P("tm", None, "floor"), check_vma=False
    )
```

profile of v0, /device:TPU:6, one launch (start us, length us, event | category | flops | bytes accessed | tf_op | source)
XLA Modules:
  0.0 28.0 jit_solution(11282581036022915950)
XLA Ops:
  0.0 26.7 %shard_map.28 = bf16[1,16,128]{2,1,0:T(8,128)(2,1)} custom-call(bf16[1,16,8192]{2,1,0:T(8,128)(2,1)} %x_hbm.1, bf16[1,512,8192]{2,1,0:T(8,128)(2,1)} %op_hbm.1), custom_call_target="tpu_custom_call" | custom-call | tf_op jit(solution)/shard_map/pallas_call | solution.py:321
  26.7 1.3 %copy.4 = bf16[1,16,128]{2,1,0:T(8,128)(2,1)} copy(bf16[1,16,128]{2,1,0:T(8,128)(2,1)} %shard_map.28) | data formatting | bytes 8192
where the time goes:
time: 28.2 us; the launch traced here: 28 us
  Pallas kernels  26.7 us (95%)
  local copies, waits for them, and re-layouts  1.28 us (5%)
    pallas_call x1, Pallas kernels, local(): pl.pallas_call(functools.partial(kernel, n, m, chunks), out_shape=jax.Sha...  26.7 us
    unnamed x1, local copies, waits for them, and re-layouts  1.28 us

commit v1 on v0

--- a/solution.py
+++ b/solution.py
@@ -9,6 +9,7 @@
 
 MESH = pl.DeviceIdType.MESH
 LOOK = 1
+AHEAD = 2
 
 
 def each(low, high, body):
@@ -310,17 +311,421 @@
         to_floor(step).wait_send()
 
 
+def square(
+    m, chunks, split, x_hbm, op_hbm, out_ref, x, op, acc, part, total, share,
+    own_sem, op_sem, x_sem, y_sem, pair_sem, pass_sem, fwd_sem, in_sem,
+    red_out, red_in, floor_out, floor_in, hello,
+):
+    n = part.shape[0]
+    chips = n // 2
+    half = chunks // 2
+    me, floor = lax.axis_index("tm"), lax.axis_index("floor")
+    chip, core = lax.div(me, 2), lax.rem(me, 2)
+    row, col = lax.div(chip, 2), lax.rem(chip, 2)
+    sources = [chip, 2 * row + 1 - col, 2 * (1 - row) + col, 2 * (1 - row) + 1 - col]
+    pair, at_x, at_y = 2 * chip + 1 - core, 2 * sources[1] + core, 2 * sources[2] + core
+    k, width = x.shape[2], x.shape[3]
+    share_size = op.shape[1] // m
+    first = chip == 0
+
+    def columns(c):
+        return pl.ds(pl.multiple_of(c * width, width), width)
+
+    def own(c):
+        return pltpu.make_async_copy(x_hbm.at[0, :, columns(c)], x.at[c, core], own_sem.at[c])
+
+    def weights(c):
+        return pltpu.make_async_copy(op_hbm.at[0, :, columns(c)], op.at[c], op_sem.at[c])
+
+    def order(p):
+        paired = lax.rem(p, 2) * half + lax.div(p, 2)
+        return jnp.where((chip == 0) | (chip == chips - 1), paired, lax.rem(p + split, chunks))
+
+    for c in range(chunks):
+        own(c).start()
+        weights(c).start()
+
+    def greet(sem):
+        for target in (pair, at_x, at_y):
+            pl.semaphore_signal(sem, inc=1, device_id={"tm": target}, device_id_type=MESH)
+
+        @pl.when(floor > 0)
+        def _():
+            pl.semaphore_signal(sem, inc=1, device_id={"floor": floor - 1}, device_id_type=MESH)
+
+        @pl.when(floor < m - 1)
+        def _():
+            pl.semaphore_signal(sem, inc=1, device_id={"floor": floor + 1}, device_id_type=MESH)
+
+    greeted = 3 + jnp.where(floor > 0, 1, 0) + jnp.where(floor < m - 1, 1, 0)
+    barrier = pltpu.get_barrier_semaphore()
+    greet(barrier)
+    pl.semaphore_wait(barrier, greeted)
+
+    def need(source, at):
+        return source + at < chips
+
+    needs = [need(source, chip) for source in sources]
+
+    def by_x(source, c):
+        outer = (source == 0) | (source == chips - 1)
+        return (outer & (c < half)) | ((source == 1) & (c < split)) | ((source == 2) & (c >= split))
+
+    def to_x(source, across_x, c):
+        return need(source, across_x) | by_x(source, c)
+
+    def to_y(source, across_y, c):
+        return need(source, across_y) | jnp.logical_not(by_x(source, c))
+
+    def send(c, slot, target, sem, into, source=None):
+        return pltpu.make_async_remote_copy(
+            src_ref=x.at[c, slot] if source is None else source,
+            dst_ref=x.at[c, into], send_sem=sem, recv_sem=in_sem.at[c, into],
+            device_id={"tm": target}, device_id_type=MESH,
+        )
+
+    def mine(c):
+        return x_hbm.at[0, :, columns(c)]
+
+    def send_x(c, act):
+        @pl.when(to_x(chip, sources[1], c))
+        def _():
+            act(send(c, core, at_x, x_sem.at[c], 2 + core, mine(c)))
+
+    def send_y(c, act):
+        @pl.when(to_y(chip, sources[2], c))
+        def _():
+            act(send(c, core, at_y, y_sem.at[c], 4 + core, mine(c)))
+
+    def send_pair(c, act):
+        @pl.when(needs[0])
+        def _():
+            act(send(c, core, pair, pair_sem.at[c], core, mine(c)))
+
+    def start(copy):
+        copy.start()
+
+    def wait_send(copy):
+        copy.wait_send()
+
+    def wait_recv(copy):
+        copy.wait_recv()
+
+    def forward(c, near, act):
+        act(send(c, 2 * near + core, pair, fwd_sem.at[near, c], 2 * near + core))
+
+    def taken_x(c):
+        return to_x(sources[1], chip, c)
+
+    def taken_y(c):
+        return to_y(sources[2], chip, c)
+
+    def pass_x(c, act):
+        @pl.when(by_x(sources[1], c))
+        def _():
+            act(send(c, 2 + core, at_y, pass_sem.at[0, c], 6 + core))
+
+    def pass_y(c, act):
+        @pl.when(jnp.logical_not(by_x(sources[2], c)))
+        def _():
+            act(send(c, 4 + core, at_x, pass_sem.at[1, c], 6 + core))
+
+    late_x, late_y = chip == 1, chip == 2
+
+    def first_half(c, _):
+        send_x(c, start)
+        send_y(c, start)
+        return 0
+
+    def second_half(c, _):
+        @pl.when(jnp.logical_not(late_x))
+        def _():
+            send_x(c, start)
+
+        @pl.when(jnp.logical_not(late_y))
+        def _():
+            send_y(c, start)
+
+        return 0
+
+    lax.fori_loop(0, half, first_half, 0)
+    lax.fori_loop(half, chunks, second_half, 0)
+
+    def all_pairs(c, _):
+        send_pair(c, start)
+        return 0
+
+    lax.fori_loop(0, chunks, all_pairs, 0)
+    greet(hello.at[0])
+    acc[...] = jnp.zeros_like(acc)
+
+    steps = 2 * chunks
+
+    def near_step(step):
+        return jnp.where(first, (step < half) | (step >= half + chunks), step < chunks)
+
+    def near_chunk(step):
+        return jnp.where(first & (step >= half), step - chunks, step)
+
+    def far_chunk(step):
+        return order(jnp.where(first, step - half, step - chunks))
+
+    def arrive(step):
+        near = near_step(step)
+
+        @pl.when(near)
+        def _():
+            c = near_chunk(step)
+            at = jnp.where(chip == 1, lax.rem(c + half, chunks), c)
+
+            @pl.when(taken_y(at))
+            def _():
+                send(at, 0, pair, in_sem.at[0, 0], 4 + core).wait_recv()
+                pass_y(at, start)
+
+            @pl.when(taken_x(c))
+            def _():
+                send(c, 0, pair, in_sem.at[0, 0], 2 + core).wait_recv()
+                pass_x(c, start)
+
+            @pl.when(needs[1])
+            def _():
+                forward(c, 1, start)
+
+            @pl.when(needs[2])
+            def _():
+                forward(at, 2, start)
+
+            @pl.when(c == half - 1)
+            def _():
+                def late(i, _):
+                    @pl.when(late_x)
+                    def _():
+                        send_x(i, start)
+
+                    @pl.when(late_y)
+                    def _():
+                        send_y(i, start)
+
+                    return 0
+
+                lax.fori_loop(half, chunks, late, 0)
+
+        @pl.when(jnp.logical_not(near))
+        def _():
+            c = far_chunk(step)
+            send(c, 0, pair, in_sem.at[0, 0], 6 + core).wait_recv()
+            forward(c, 3, start)
+
+    def image_of(rows, c):
+        return lax.dot_general(
+            rows.reshape(-1, width), op[c], (((1,), (1,)), ((), ())), preferred_element_type=jnp.float32
+        ).reshape(-1, k, op.shape[1])
+
+    spare = 2 * len(sources)
+
+    def compute(step):
+        near = near_step(step)
+        other = 1 - core
+
+        def prepare(c):
+            own(c).wait()
+            weights(c).wait()
+
+            @pl.when(needs[0])
+            def _():
+                send(c, 0, pair, in_sem.at[0, 0], other).wait_recv()
+
+        @pl.when(near)
+        def _():
+            c = near_chunk(step)
+            held = first & (c >= half)
+
+            @pl.when(jnp.logical_not(held))
+            def _():
+                prepare(c)
+
+            for at in (1, 2):
+                @pl.when(needs[at])
+                def _(at=at):
+                    send(c, 0, pair, in_sem.at[0, 0], 2 * at + other).wait_recv()
+
+            @pl.when(needs[0] | needs[1] | needs[2])
+            def _():
+                image = image_of(x[c, 0:6], c)
+                slot = jnp.where(held, spare, 0)
+                acc[pl.ds(slot, 2)] += image[0:2]
+                acc[2:6] += image[2:6]
+
+        @pl.when(jnp.logical_not(near))
+        def _():
+            c = far_chunk(step)
+            held = first & (c >= half)
+
+            @pl.when(held)
+            def _():
+                prepare(c)
+
+            send(c, 0, pair, in_sem.at[0, 0], 6 + other).wait_recv()
+            image = image_of(jnp.concatenate([x[c, 0:2], x[c, 6:8]], axis=0), c)
+            slot = jnp.where(held, 0, spare)
+            acc[pl.ds(slot, 2)] += image[0:2]
+            acc[6:8] += image[2:4]
+
+    def lag_part(slot, act):
+        block = 2 * sources[slot // 2] + slot % 2
+
+        @pl.when((block > 0) & (block + me < n))
+        def _():
+            act(pltpu.make_async_remote_copy(
+                src_ref=acc.at[slot], dst_ref=part.at[me],
+                send_sem=red_out.at[slot], recv_sem=red_in.at[me],
+                device_id={"tm": jnp.minimum(block + me, n - 1)}, device_id_type=MESH,
+            ))
+
+    def lag_parts(early, act):
+        for at in (3, 1, 2, 0):
+            now = {0: early, 3: first == early}.get(at, first != early)
+            if at == 0 and not early:
+                continue
+
+            @pl.when(now)
+            def _(at=at):
+                for j in (0, 1):
+                    lag_part(2 * at + j, act)
+
+    for step in range(AHEAD):
+        arrive(step)
+    pl.semaphore_wait(hello.at[0], greeted)
+    greet(hello.at[1])
+    flush = jnp.where(first, half + chunks - 1, chunks - 1)
+
+    def body(step, _):
+        @pl.when(step + AHEAD < steps)
+        def _():
+            arrive(step + AHEAD)
+
+        compute(step)
+
+        @pl.when(step == flush)
+        def _():
+            pl.semaphore_wait(hello.at[1], greeted)
+            lag_parts(True, start)
+
+        return 0
+
+    lax.fori_loop(0, steps, body, 0)
+    lag_parts(False, start)
+
+    def drain(c, _):
+        send_x(c, wait_send)
+        send_y(c, wait_send)
+        send_pair(c, wait_send)
+
+        @pl.when(taken_x(c))
+        def _():
+            pass_x(c, wait_send)
+
+        @pl.when(taken_y(c))
+        def _():
+            pass_y(c, wait_send)
+
+        for at in (1, 2, 3):
+            @pl.when(needs[at])
+            def _(at=at):
+                forward(c, at, wait_send)
+
+        return 0
+
+    lax.fori_loop(0, chunks, drain, 0)
+
+    def add_lag(i, value):
+        lag = me - 1 - i
+        pltpu.make_async_remote_copy(
+            src_ref=acc.at[0], dst_ref=part.at[lag],
+            send_sem=red_out.at[0], recv_sem=red_in.at[lag],
+            device_id={"tm": pair}, device_id_type=MESH,
+        ).wait_recv()
+        return value + part[lag]
+
+    value = lax.fori_loop(0, me, add_lag, acc[2 * chip])
+    for j in range(m):
+        total[j] = value[:, j * share_size:(j + 1) * share_size]
+
+    def to_floor(other, act):
+        act(pltpu.make_async_remote_copy(
+            src_ref=total.at[other], dst_ref=share.at[floor],
+            send_sem=floor_out.at[other], recv_sem=floor_in.at[floor],
+            device_id={"floor": other}, device_id_type=MESH,
+        ))
+
+    def each_floor(act):
+        for step in range(m - 1, 0, -1):
+            @pl.when(floor + step < m)
+            def _(step=step):
+                act(floor + step)
+
+            @pl.when(floor - step >= 0)
+            def _(step=step):
+                act(floor - step)
+
+    each_floor(lambda other: to_floor(other, start))
+    result = total[floor]
+    for step in range(1, m):
+        source = lax.rem(floor + step, m)
+        pltpu.make_async_remote_copy(
+            src_ref=total.at[source], dst_ref=share.at[source],
+            send_sem=floor_out.at[source], recv_sem=floor_in.at[source],
+            device_id={"floor": source}, device_id_type=MESH,
+        ).wait_recv()
+        result = result + share[source]
+    out_ref[0] = result.astype(out_ref.dtype)
+
+    lag_parts(True, wait_send)
+    lag_parts(False, wait_send)
+    each_floor(lambda other: to_floor(other, wait_send))
+
+
+def square_call(n, m, samples, operator):
+    _, k, depth = samples.shape
+    sensors = operator.shape[1]
+    chunks = 8
+    width = depth // chunks
+    dma = pltpu.SemaphoreType.DMA
+    return pl.pallas_call(
+        functools.partial(square, m, chunks, chunks // 4),
+        out_shape=pltpu.VMEM((1, k, sensors // m), jnp.bfloat16),
+        in_specs=[pl.BlockSpec(memory_space=pl.ANY)] * 2,
+        out_specs=pl.BlockSpec(memory_space=pltpu.VMEM),
+        scratch_shapes=[
+            pltpu.VMEM((chunks, n, k, width), jnp.bfloat16),
+            pltpu.VMEM((chunks, sensors, width), jnp.bfloat16),
+            pltpu.VMEM((n + 2, k, sensors), jnp.float32),
+            pltpu.VMEM((n, k, sensors), jnp.float32),
+            pltpu.VMEM((m, k, sensors // m), jnp.float32),
+            pltpu.VMEM((m, k, sensors // m), jnp.float32),
+            dma((chunks,)), dma((chunks,)), dma((chunks,)), dma((chunks,)), dma((chunks,)),
+            dma((2, chunks)), dma((4, chunks)), dma((chunks, n)),
+            dma((n,)), dma((n,)), dma((m,)), dma((m,)),
+            pltpu.SemaphoreType.REGULAR((2,)),
+        ],
+        compiler_params=pltpu.CompilerParams(collective_id=0, has_side_effects=True),
+    )(samples, operator)
+
+
 def solution(mesh):
     n, m = mesh.shape["tm"], mesh.shape["floor"]
 
     def local(samples, operator):
+        if grid_of(n // 2) == (2, 2):
+            return square_call(n, m, samples, operator)
         _, k, depth = samples.shape
         sensors = operator.shape[1]
         chunks = 4
         width = depth // chunks
         return pl.pallas_call(
             functools.partial(kernel, n, m, chunks),
-            out_shape=jax.ShapeDtypeStruct((1, k, sensors // m), jnp.bfloat16),
+            out_shape=pltpu.VMEM((1, k, sensors // m), jnp.bfloat16),
             in_specs=[pl.BlockSpec(memory_space=pl.ANY)] * 2,
             out_specs=pl.BlockSpec(memory_space=pltpu.VMEM),
             scratch_shapes=[

time: 28.2 us -> 25.9 us (0.918)
  the two profiles are of different devices: /device:TPU:6 before, /device:TPU:2 now
where the time goes in v1:
time: 25.9 us; the launch traced here: 25.7 us
  Pallas kernels  25.1 us (97%)
  local copies, waits for them, and re-layouts  0.6 us (2%)
    pallas_call x1, Pallas kernels, square_call(): pl.pallas_call(functools.partial(square, m, chunks, chunks // 4), out_sha...  25.1 us
    unnamed x1, local copies, waits for them, and re-layouts  0.6 us

profile of v1, /device:TPU:2, one launch (start us, length us, event | category | flops | bytes accessed | tf_op | source)
XLA Modules:
  0.0 25.7 jit_solution(8995132373671307992)
XLA Ops:
  0.0 25.1 %shard_map.28 = bf16[1,16,128]{2,1,0:T(8,128)(2,1)S(1)} custom-call(bf16[1,16,8192]{2,1,0:T(8,128)(2,1)} %x_hbm.1, bf16[1,512,8192]{2,1,0:T(8,128)(2,1)} %op_hbm.1), custom_call_target="tpu_custom_call" | custom-call | tf_op jit(solution)/shard_map/pallas_call | solution.py:695
  25.1 0.6 %copy.4 = bf16[1,16,128]{2,1,0:T(8,128)(2,1)} copy(bf16[1,16,128]{2,1,0:T(8,128)(2,1)S(1)} %shard_map.28) | data formatting | bytes 8192

commit v2 on v0

--- a/solution.py
+++ b/solution.py
@@ -310,17 +310,334 @@
         to_floor(step).wait_send()
 
 
+def square(
+    m, chunks, split, x_hbm, op_hbm, out_ref, x, mine, op, acc, sums, part, total, share,
+    own_sem, mine_sem, op_sem, swap_out, swap_in, pair_sem, x_sem, y_sem, pass_sem, in_sem,
+    red_out, red_in, floor_out, floor_in, hello,
+):
+    n = part.shape[0]
+    chips = n // 2
+    me, floor = lax.axis_index("tm"), lax.axis_index("floor")
+    chip, core = lax.div(me, 2), lax.rem(me, 2)
+    row, col = lax.div(chip, 2), lax.rem(chip, 2)
+    sources = [chip, 2 * row + 1 - col, 2 * (1 - row) + col, 2 * (1 - row) + 1 - col]
+    other = 1 - core
+    pair = 2 * chip + other
+    k, width = x.shape[2], x.shape[3]
+    sensors = op.shape[2]
+    share_size = sensors // m
+    inner = (chip == 1) | (chip == 2)
+
+    def columns(half, j):
+        return pl.ds(pl.multiple_of((half * chunks + j) * width, width), width)
+
+    def own(j):
+        return pltpu.make_async_copy(x_hbm.at[0, :, columns(core, j)], x.at[j, core], own_sem.at[j])
+
+    def staged(half, j):
+        return pltpu.make_async_copy(x_hbm.at[0, :, columns(half, j)], mine.at[half, j], mine_sem.at[half, j])
+
+    def weights(j):
+        return pltpu.make_async_copy(op_hbm.at[0, :, columns(core, j)], op.at[j, core], op_sem.at[j])
+
+    for j in range(chunks):
+        for half in (0, 1):
+            staged(half, j).start()
+    for j in range(chunks):
+        own(j).start()
+
+    def greet(sem):
+        for target in (pair, 2 * sources[1], 2 * sources[1] + 1, 2 * sources[2], 2 * sources[2] + 1):
+            pl.semaphore_signal(sem, inc=1, device_id={"tm": target}, device_id_type=MESH)
+
+        @pl.when(floor > 0)
+        def _():
+            pl.semaphore_signal(sem, inc=1, device_id={"floor": floor - 1}, device_id_type=MESH)
+
+        @pl.when(floor < m - 1)
+        def _():
+            pl.semaphore_signal(sem, inc=1, device_id={"floor": floor + 1}, device_id_type=MESH)
+
+    greeted = 5 + jnp.where(floor > 0, 1, 0) + jnp.where(floor < m - 1, 1, 0)
+    barrier = pltpu.get_barrier_semaphore()
+    greet(barrier)
+    pl.semaphore_wait(barrier, greeted)
+
+    def need(source, at):
+        return source + at < chips
+
+    needs = [need(source, chip) for source in sources]
+
+    def by_x(source, parity, j):
+        outer = (source == 0) | (source == chips - 1)
+        through_first = jnp.where(source == 1, j < split, j >= split)
+        return (outer & (parity == j % 2)) | (jnp.logical_not(outer) & through_first)
+
+    def remote(src, dst, out, into, target):
+        return pltpu.make_async_remote_copy(
+            src_ref=src, dst_ref=dst, send_sem=out, recv_sem=into, device_id={"tm": target}, device_id_type=MESH
+        )
+
+    def start(copy):
+        copy.start()
+
+    def wait_send(copy):
+        copy.wait_send()
+
+    def send_x(j, act):
+        @pl.when(needs_at_x | by_x(chip, core, j))
+        def _():
+            for half in (0, 1):
+                act(remote(mine.at[half, j], x.at[j, 2 + core], x_sem.at[half, j], in_sem.at[j, 2 + core], 2 * sources[1] + half))
+
+    def send_y(j, act):
+        @pl.when(needs_at_y | jnp.logical_not(by_x(chip, core, j)))
+        def _():
+            for half in (0, 1):
+                act(remote(mine.at[half, j], x.at[j, 4 + core], y_sem.at[half, j], in_sem.at[j, 4 + core], 2 * sources[2] + half))
+
+    needs_at_x, needs_at_y = need(chip, sources[1]), need(chip, sources[2])
+
+    def send_pair(j, act):
+        act(remote(mine.at[other, j], x.at[j, core], pair_sem.at[j], in_sem.at[j, core], pair))
+
+    def swap(j, act):
+        act(remote(op_hbm.at[0, :, columns(other, j)], op.at[j, core], swap_out.at[j], swap_in.at[j], pair))
+
+    def swapped(j):
+        remote(op.at[j, core], op.at[j, other], swap_out.at[j], swap_in.at[j], pair).wait_recv()
+
+    def taken(j, slot):
+        remote(x.at[j, slot], x.at[j, slot], pair_sem.at[j], in_sem.at[j, slot], pair).wait_recv()
+
+    def pass_x(j, parity, act):
+        act(remote(x.at[j, 2 + parity], x.at[j, 6 + parity], pass_sem.at[0, parity, j], in_sem.at[j, 6 + parity], 2 * sources[2] + core))
+
+    def pass_y(j, parity, act):
+        act(remote(x.at[j, 4 + parity], x.at[j, 6 + parity], pass_sem.at[1, parity, j], in_sem.at[j, 6 + parity], 2 * sources[1] + core))
+
+    def from_x(j, here, wait, act):
+        for parity in (0, 1):
+            onward = by_x(sources[1], parity, j)
+
+            @pl.when(here & (needs[1] | onward))
+            def _(parity=parity, onward=onward):
+                if wait:
+                    taken(j, 2 + parity)
+
+                @pl.when(onward)
+                def _():
+                    pass_x(j, parity, act)
+
+    def from_y(j, here, wait, act):
+        for parity in (0, 1):
+            onward = jnp.logical_not(by_x(sources[2], parity, j))
+
+            @pl.when(here & (needs[2] | onward))
+            def _(parity=parity, onward=onward):
+                if wait:
+                    taken(j, 4 + parity)
+
+                @pl.when(onward)
+                def _():
+                    pass_y(j, parity, act)
+
+    lead = chunks // 2
+    for j in range(chunks):
+        for half in (0, 1):
+            staged(half, j).wait()
+
+        @pl.when((j < lead) | jnp.logical_not(needs_at_x))
+        def _(j=j):
+            send_x(j, start)
+
+        @pl.when((j < lead) | jnp.logical_not(needs_at_y))
+        def _(j=j):
+            send_y(j, start)
+
+    for j in range(chunks):
+        weights(j).start()
+        send_pair(j, start)
+        swap(j, start)
+    greet(hello.at[0])
+
+    def send_late(j):
+        @pl.when(needs_at_x)
+        def _():
+            send_x(j, start)
+
+        @pl.when(needs_at_y)
+        def _():
+            send_y(j, start)
+
+    for j in range(chunks):
+        from_x(j, jnp.logical_not(needs[1]), True, start)
+        from_y(j, jnp.logical_not(needs[2]), True, start)
+        if j + lead < chunks:
+            @pl.when(inner)
+            def _(j=j):
+                send_late(j + lead)
+
+    pl.semaphore_wait(hello.at[0], greeted)
+    greet(hello.at[1])
+
+    def arrive(j):
+        from_x(j, needs[1], True, start)
+        from_y(j, needs[2], True, start)
+        if j == split - 1:
+            @pl.when(jnp.logical_not(inner))
+            def _():
+                for late in range(lead, chunks):
+                    send_late(late)
+
+    def compute(j):
+        own(j).wait()
+        weights(j).wait()
+        taken(j, other)
+        swapped(j)
+        for parity in (0, 1):
+            taken(j, 6 + parity)
+        image = lax.dot_general(
+            x[j].reshape(-1, width), op[j].reshape(-1, width), (((1,), (1,)), ((), ())),
+            preferred_element_type=jnp.float32,
+        ).reshape(-1, k, 2 * sensors)
+        if j == 0:
+            acc[...] = image
+        else:
+            acc[...] += image
+
+    arrive(0)
+    for j in range(chunks):
+        if j + 1 < chunks:
+            arrive(j + 1)
+        compute(j)
+
+    pl.semaphore_wait(hello.at[1], greeted)
+
+    def slot_of(block):
+        source = block // 2
+        across = jnp.where(col == source % 2, 0, 2) + jnp.where(row == source // 2, 0, 4)
+        return across + block % 2
+
+    def record(u, act):
+        act(pltpu.make_async_remote_copy(
+            src_ref=sums.at[u], dst_ref=part.at[me], send_sem=red_out.at[u], recv_sem=red_in.at[me],
+            device_id={"tm": jnp.minimum(2 * chip + u, n - 1)}, device_id_type=MESH,
+        ))
+
+    def records(act, add):
+        for u in range(n - 1, -1, -1):
+            @pl.when(2 * chip + u < n)
+            def _(u=u):
+                if add:
+                    value = acc[slot_of(u), :, :sensors]
+                    if u > 0:
+                        value = value + acc[slot_of(u - 1), :, sensors:]
+                    sums[u] = value
+                if u > 1:
+                    record(u, act)
+                else:
+                    @pl.when(core != u)
+                    def _():
+                        record(u, act)
+
+    records(start, True)
+
+    for j in range(chunks):
+        send_x(j, wait_send)
+        send_y(j, wait_send)
+        send_pair(j, wait_send)
+        swap(j, wait_send)
+        from_x(j, True, False, wait_send)
+        from_y(j, True, False, wait_send)
+
+    def add_part(i, value):
+        sender = jnp.where(i == 0, pair, 2 * chip - i)
+        pltpu.make_async_remote_copy(
+            src_ref=sums.at[0], dst_ref=part.at[sender], send_sem=red_out.at[0], recv_sem=red_in.at[sender],
+            device_id={"tm": pair}, device_id_type=MESH,
+        ).wait_recv()
+        return value + part[sender]
+
+    value = lax.fori_loop(0, 2 * chip + 1, add_part, sums[core])
+    for j in range(m):
+        total[j] = value[:, j * share_size:(j + 1) * share_size]
+
+    def to_floor(other, act):
+        act(pltpu.make_async_remote_copy(
+            src_ref=total.at[other], dst_ref=share.at[floor],
+            send_sem=floor_out.at[other], recv_sem=floor_in.at[floor],
+            device_id={"floor": other}, device_id_type=MESH,
+        ))
+
+    def each_floor(act):
+        for step in range(m - 1, 0, -1):
+            @pl.when(floor + step < m)
+            def _(step=step):
+                act(floor + step)
+
+            @pl.when(floor - step >= 0)
+            def _(step=step):
+                act(floor - step)
+
+    each_floor(lambda other: to_floor(other, start))
+    result = total[floor]
+    for step in range(1, m):
+        source = lax.rem(floor + step, m)
+        pltpu.make_async_remote_copy(
+            src_ref=total.at[source], dst_ref=share.at[source],
+            send_sem=floor_out.at[source], recv_sem=floor_in.at[source],
+            device_id={"floor": source}, device_id_type=MESH,
+        ).wait_recv()
+        result = result + share[source]
+    out_ref[0] = result.astype(out_ref.dtype)
+
+    records(wait_send, False)
+    each_floor(lambda other: to_floor(other, wait_send))
+
+
+def square_call(n, m, samples, operator):
+    _, k, depth = samples.shape
+    sensors = operator.shape[1]
+    chunks = 4
+    width = depth // (2 * chunks)
+    dma = pltpu.SemaphoreType.DMA
+    return pl.pallas_call(
+        functools.partial(square, m, chunks, 1),
+        out_shape=pltpu.VMEM((1, k, sensors // m), jnp.bfloat16),
+        in_specs=[pl.BlockSpec(memory_space=pl.ANY)] * 2,
+        out_specs=pl.BlockSpec(memory_space=pltpu.VMEM),
+        scratch_shapes=[
+            pltpu.VMEM((chunks, n, k, width), jnp.bfloat16),
+            pltpu.VMEM((2, chunks, k, width), jnp.bfloat16),
+            pltpu.VMEM((chunks, 2, sensors, width), jnp.bfloat16),
+            pltpu.VMEM((n, k, 2 * sensors), jnp.float32),
+            pltpu.VMEM((n, k, sensors), jnp.float32),
+            pltpu.VMEM((n, k, sensors), jnp.float32),
+            pltpu.VMEM((m, k, sensors // m), jnp.float32),
+            pltpu.VMEM((m, k, sensors // m), jnp.float32),
+            dma((chunks,)), dma((2, chunks)), dma((chunks,)), dma((chunks,)), dma((chunks,)), dma((chunks,)),
+            dma((2, chunks)), dma((2, chunks)), dma((2, 2, chunks)), dma((chunks, n)),
+            dma((n,)), dma((n,)), dma((m,)), dma((m,)),
+            pltpu.SemaphoreType.REGULAR((2,)),
+        ],
+        compiler_params=pltpu.CompilerParams(collective_id=0, has_side_effects=True),
+    )(samples, operator)
+
+
 def solution(mesh):
     n, m = mesh.shape["tm"], mesh.shape["floor"]
 
     def local(samples, operator):
+        if grid_of(n // 2) == (2, 2):
+            return square_call(n, m, samples, operator)
         _, k, depth = samples.shape
         sensors = operator.shape[1]
         chunks = 4
         width = depth // chunks
         return pl.pallas_call(
             functools.partial(kernel, n, m, chunks),
-            out_shape=jax.ShapeDtypeStruct((1, k, sensors // m), jnp.bfloat16),
+            out_shape=pltpu.VMEM((1, k, sensors // m), jnp.bfloat16),
             in_specs=[pl.BlockSpec(memory_space=pl.ANY)] * 2,
             out_specs=pl.BlockSpec(memory_space=pltpu.VMEM),
             scratch_shapes=[

time: 28.2 us -> 25.4 us (0.901)
  the two profiles are of different devices: /device:TPU:6 before, /device:TPU:2 now
where the time goes in v2:
time: 25.4 us; the launch traced here: 25.3 us
  Pallas kernels  24.7 us (97%)
  local copies, waits for them, and re-layouts  0.6 us (2%)
    pallas_call x1, Pallas kernels, square_call(): pl.pallas_call(functools.partial(square, m, chunks, 1), out_shape=pltpu.V...  24.7 us
    unnamed x1, local copies, waits for them, and re-layouts  0.6 us

profile of v2, /device:TPU:2, one launch (start us, length us, event | category | flops | bytes accessed | tf_op | source)
XLA Modules:
  0.0 25.3 jit_solution(8337139477541731660)
XLA Ops:
  0.0 24.7 %shard_map.28 = bf16[1,16,128]{2,1,0:T(8,128)(2,1)S(1)} custom-call(bf16[1,16,8192]{2,1,0:T(8,128)(2,1)} %x_hbm.1, bf16[1,512,8192]{2,1,0:T(8,128)(2,1)} %op_hbm.1), custom_call_target="tpu_custom_call" | custom-call | tf_op jit(solution)/shard_map/pallas_call | solution.py:605
  24.7 0.6 %copy.4 = bf16[1,16,128]{2,1,0:T(8,128)(2,1)} copy(bf16[1,16,128]{2,1,0:T(8,128)(2,1)S(1)} %shard_map.28) | data formatting | bytes 8192

commit v3 on v0

--- a/solution.py
+++ b/solution.py
@@ -310,17 +310,429 @@
         to_floor(step).wait_send()
 
 
+def square(
+    m, widths, split, x_hbm, op_hbm, out_ref, x, mine, op, acc, sums, part, total, share,
+    load_sem, swap_in, pair_in, in_sem, sent, red_in, floor_in, hello,
+):
+    n = part.shape[0]
+    chips = n // 2
+    me, floor = lax.axis_index("tm"), lax.axis_index("floor")
+    chip, core = lax.div(me, 2), lax.rem(me, 2)
+    row, col = lax.div(chip, 2), lax.rem(chip, 2)
+    sources = [chip, 2 * row + 1 - col, 2 * (1 - row) + col, 2 * (1 - row) + 1 - col]
+    other = 1 - core
+    pair = 2 * chip + other
+    chunks, starts = len(widths), [sum(widths[:j]) for j in range(len(widths))]
+    k, depth = x.shape[1], x.shape[2]
+    sensors = op.shape[1]
+    share_size = sensors // m
+    inner = (chip == 1) | (chip == 2)
+
+    def columns(half, j):
+        begin, size = (starts[j], widths[j]) if isinstance(j, int) else (j * widths[0], widths[0])
+        return pl.ds(pl.multiple_of(half * depth + begin, 128), size)
+
+    def at(j):
+        if isinstance(j, int):
+            return slice(starts[j], starts[j] + widths[j])
+        return pl.ds(pl.multiple_of(j * widths[0], 128), widths[0])
+
+    own = pltpu.make_async_copy(x_hbm.at[0, :, pl.ds(pl.multiple_of(core * depth, 128), depth)], x.at[core], load_sem.at[0])
+    staged = pltpu.make_async_copy(x_hbm.at[0], mine, load_sem.at[1])
+    weights = pltpu.make_async_copy(
+        op_hbm.at[0, :, pl.ds(pl.multiple_of(core * depth, 128), depth)], op.at[core], load_sem.at[2]
+    )
+    staged.start()
+    own.start()
+
+    neighbours = (2 * sources[1], 2 * sources[1] + 1, 2 * sources[2], 2 * sources[2] + 1)
+
+    def greet(sem, all_round):
+        pl.semaphore_signal(sem, inc=1, device_id={"tm": pair}, device_id_type=MESH)
+
+        @pl.when(all_round)
+        def _():
+            for target in neighbours:
+                pl.semaphore_signal(sem, inc=1, device_id={"tm": target}, device_id_type=MESH)
+
+        @pl.when(floor > 0)
+        def _():
+            pl.semaphore_signal(sem, inc=1, device_id={"floor": floor - 1}, device_id_type=MESH)
+
+        @pl.when(floor < m - 1)
+        def _():
+            pl.semaphore_signal(sem, inc=1, device_id={"floor": floor + 1}, device_id_type=MESH)
+
+    beside = jnp.where(floor > 0, 1, 0) + jnp.where(floor < m - 1, 1, 0)
+    greeted = 5 + beside
+    barrier = pltpu.get_barrier_semaphore()
+    greet(barrier, chip < chips - 1)
+    pl.semaphore_wait(barrier, jnp.where(inner, 3, 5) + beside)
+
+    @pl.when(chip == chips - 1)
+    def _():
+        for target in neighbours:
+            pl.semaphore_signal(hello.at[2], inc=1, device_id={"tm": target}, device_id_type=MESH)
+
+    def need(source, at):
+        return source + at < chips
+
+    needs = [need(source, chip) for source in sources]
+
+    def by_x(source, parity, j):
+        outer = (source == 0) | (source == chips - 1)
+        through_first = jnp.where(source == 1, j < split, j >= split)
+        return (outer & (parity == j % 2)) | (jnp.logical_not(outer) & through_first)
+
+    def remote(src, dst, out, into, target):
+        return pltpu.make_async_remote_copy(
+            src_ref=src, dst_ref=dst, send_sem=out, recv_sem=into, device_id={"tm": target}, device_id_type=MESH
+        )
+
+    def start(copy):
+        copy.start()
+
+    def wait_send(copy):
+        copy.wait_send()
+
+    def send_x(j, act):
+        @pl.when(needs_at_x | by_x(chip, core, j))
+        def _():
+            for half in (0, 1):
+                act(remote(mine.at[:, columns(half, j)], x.at[2 + core, :, at(j)], sent.at[0], in_sem.at[1, j], 2 * sources[1] + half))
+
+    def send_y(j, act):
+        @pl.when(needs_at_y | jnp.logical_not(by_x(chip, core, j)))
+        def _():
+            for half in (0, 1):
+                act(remote(mine.at[:, columns(half, j)], x.at[4 + core, :, at(j)], sent.at[0], in_sem.at[2, j], 2 * sources[2] + half))
+
+    needs_at_x, needs_at_y = need(chip, sources[1]), need(chip, sources[2])
+
+    def send_pair(act):
+        there = pl.ds(pl.multiple_of(other * depth, 128), depth)
+        act(remote(mine.at[:, there], x.at[core], sent.at[0], pair_in.at[0], pair))
+
+    parts = (slice(0, starts[2]), slice(starts[2], depth))
+
+    def swap(p, act):
+        begin, size = parts[p].start, parts[p].stop - parts[p].start
+        there = pl.ds(pl.multiple_of(other * depth + begin, 128), size)
+        act(remote(op_hbm.at[0, :, there], op.at[core, :, parts[p]], sent.at[0], swap_in.at[p], pair))
+
+    def swapped(p):
+        remote(op.at[core, :, parts[p]], op.at[other, :, parts[p]], sent.at[0], swap_in.at[p], pair).wait_recv()
+
+    def taken(source, j, blocks):
+        here = x.at[2 * source:2 * source + blocks, :, at(j)]
+        remote(here, here, sent.at[0], in_sem.at[source, j], pair).wait_recv()
+
+    def pass_x(j, parity, act):
+        act(remote(x.at[2 + parity, :, at(j)], x.at[6 + parity, :, at(j)], sent.at[0], in_sem.at[3, j], 2 * sources[2] + core))
+
+    def pass_y(j, parity, act):
+        act(remote(x.at[4 + parity, :, at(j)], x.at[6 + parity, :, at(j)], sent.at[0], in_sem.at[3, j], 2 * sources[1] + core))
+
+    def come(source, j, both, onward):
+        count = onward[0].astype(jnp.int32) + onward[1].astype(jnp.int32)
+        for blocks in (1, 2):
+            @pl.when(jnp.where(both, 2, count) == blocks)
+            def _(blocks=blocks):
+                taken(source, j, blocks)
+
+    def from_x(j, here, wait, act):
+        onward = [by_x(sources[1], parity, j) for parity in (0, 1)]
+
+        @pl.when(here)
+        def _():
+            if wait:
+                come(1, j, needs[1], onward)
+            for parity in (0, 1):
+                @pl.when(onward[parity])
+                def _(parity=parity):
+                    pass_x(j, parity, act)
+
+    def from_y(j, here, wait, act):
+        onward = [jnp.logical_not(by_x(sources[2], parity, j)) for parity in (0, 1)]
+
+        @pl.when(here)
+        def _():
+            if wait:
+                come(2, j, needs[2], onward)
+            for parity in (0, 1):
+                @pl.when(onward[parity])
+                def _(parity=parity):
+                    pass_y(j, parity, act)
+
+    lead = chunks // 2
+    staged.wait()
+    for j in range(lead):
+        @pl.when(needs_at_x)
+        def _(j=j):
+            send_x(j, start)
+
+        @pl.when(needs_at_y)
+        def _(j=j):
+            send_y(j, start)
+
+    def send_only_across():
+        for j in range(chunks):
+            @pl.when(jnp.logical_not(needs_at_x))
+            def _(j=j):
+                send_x(j, start)
+
+            @pl.when(jnp.logical_not(needs_at_y))
+            def _(j=j):
+                send_y(j, start)
+
+    @pl.when(chip == chips - 1)
+    def _():
+        send_only_across()
+
+    weights.start()
+    send_pair(start)
+    for p in (0, 1):
+        swap(p, start)
+
+    @pl.when(inner)
+    def _():
+        pl.semaphore_wait(hello.at[2], 2)
+        send_only_across()
+
+    greet(hello.at[0], True)
+
+    def send_late(j):
+        @pl.when(needs_at_x)
+        def _():
+            send_x(j, start)
+
+        @pl.when(needs_at_y)
+        def _():
+            send_y(j, start)
+
+    for j in range(chunks):
+        from_x(j, jnp.logical_not(needs[1]), True, start)
+        from_y(j, jnp.logical_not(needs[2]), True, start)
+        for late in range(lead, chunks):
+            if j == min(2 * (late - lead) + 1, chunks - 1):
+                @pl.when(inner)
+                def _(late=late):
+                    send_late(late)
+
+    pl.semaphore_wait(hello.at[0], greeted)
+    greet(hello.at[1], True)
+
+    def arrive(j):
+        from_x(j, needs[1], True, start)
+        from_y(j, needs[2], True, start)
+        if j == split - 1:
+            @pl.when(jnp.logical_not(inner))
+            def _():
+                for late in range(lead, chunks):
+                    send_late(late)
+
+    first = chip == 0
+
+    def ready(j, step):
+        if step == 0:
+            own.wait()
+            weights.wait()
+            remote(x.at[other], x.at[other], sent.at[0], pair_in.at[0], pair).wait_recv()
+            swapped(0)
+        if step == 2:
+            swapped(1)
+        taken(3, j, 2)
+
+    def multiply(j, pieces):
+        rows = jnp.concatenate([x[p, :, at(j)] for p in pieces], axis=0)
+        depth_here = rows.shape[-1]
+        return lax.dot_general(
+            rows.reshape(-1, depth_here), op[:, :, at(j)].reshape(-1, depth_here), (((1,), (1,)), ((), ())),
+            preferred_element_type=jnp.float32,
+        ).reshape(-1, k, 2 * sensors)
+
+    def compute(j, begin=False):
+        image = multiply(j, [slice(None)])
+        if begin:
+            acc[...] = image
+        else:
+            acc[...] += image
+
+    def compute_far(j):
+        image = multiply(j, [slice(0, 2), slice(6, 8)])
+        acc[0:2] += image[0:2]
+        acc[6:8] += image[2:4]
+
+    def compute_near(j):
+        acc[2:6] += multiply(j, [slice(2, 6)])
+
+    def slot_of(block):
+        source = block // 2
+        across = jnp.where(col == source % 2, 0, 2) + jnp.where(row == source // 2, 0, 4)
+        return across + block % 2
+
+    def place(i):
+        return jnp.where(2 * floor >= m, i, m - 1 - i)
+
+    def record(u, j, act):
+        act(pltpu.make_async_remote_copy(
+            src_ref=sums.at[u, j], dst_ref=part.at[me, j], send_sem=sent.at[1], recv_sem=red_in.at[j],
+            device_id={"tm": jnp.minimum(2 * chip + u, n - 1)}, device_id_type=MESH,
+        ))
+
+    def records(places, act, add):
+        def one(i, _):
+            j = place(i)
+            here = pl.ds(pl.multiple_of(j * share_size, share_size), share_size)
+            there = pl.ds(pl.multiple_of(sensors + j * share_size, share_size), share_size)
+            for u in places:
+                @pl.when(2 * chip + u < n)
+                def _(u=u):
+                    if add:
+                        value = acc[slot_of(u), :, here]
+                        if u > 0:
+                            value = value + acc[slot_of(u - 1), :, there]
+                        sums[u, j] = value
+                    if u > 1:
+                        record(u, j, act)
+                    else:
+                        @pl.when(core != u)
+                        def _():
+                            record(u, j, act)
+
+            return 0
+
+        lax.fori_loop(0, m, one, 0)
+
+    arrive(0)
+    arrive(1)
+    swapped_order = jnp.where(inner, 1, 0)
+    for step in range(chunks - 1):
+        if step > 0:
+            @pl.when(jnp.logical_not(first))
+            def _(step=step):
+                arrive(step + 1)
+
+            if step > 1:
+                @pl.when(first)
+                def _(step=step):
+                    arrive(step)
+
+        j = (swapped_order, 1 - swapped_order)[step] if step < 2 else step
+        ready(j, step)
+        compute(j, step == 0)
+
+    ready(chunks - 1, chunks - 1)
+    pl.semaphore_wait(hello.at[1], greeted)
+
+    @pl.when(first)
+    def _():
+        compute_far(chunks - 1)
+        records((7, 1, 0), start, True)
+        arrive(chunks - 1)
+        compute_near(chunks - 1)
+        records((6, 5, 3, 4, 2), start, True)
+
+    @pl.when(jnp.logical_not(first))
+    def _():
+        compute(chunks - 1)
+        records(range(n - 1, -1, -1), start, True)
+
+
+    for j in range(chunks):
+        send_x(j, wait_send)
+        send_y(j, wait_send)
+        from_x(j, True, False, wait_send)
+        from_y(j, True, False, wait_send)
+    send_pair(wait_send)
+    for p in (0, 1):
+        swap(p, wait_send)
+
+    def to_floor(other, act):
+        act(pltpu.make_async_remote_copy(
+            src_ref=total.at[other], dst_ref=share.at[floor],
+            send_sem=sent.at[2], recv_sem=floor_in.at[0],
+            device_id={"floor": other}, device_id_type=MESH,
+        ))
+
+    def gather_share(i, _):
+        j = place(i)
+
+        for c in range(chips):
+            @pl.when(chip == c)
+            def _(c=c):
+                pltpu.make_async_remote_copy(
+                    src_ref=sums.at[0:2 * c + 1, j], dst_ref=part.at[0:2 * c + 1, j], send_sem=sent.at[1],
+                    recv_sem=red_in.at[j], device_id={"tm": pair}, device_id_type=MESH,
+                ).wait_recv()
+
+        def add_part(p, value):
+            return value + part[jnp.where(p == 0, pair, 2 * chip - p), j]
+
+        total[j] = lax.fori_loop(0, 2 * chip + 1, add_part, sums[core, j])
+
+        @pl.when(j != floor)
+        def _():
+            to_floor(j, start)
+
+        return 0
+
+    lax.fori_loop(0, m, gather_share, 0)
+    records(range(n - 1, -1, -1), wait_send, False)
+    for step in range(1, m):
+        to_floor(lax.rem(floor + step, m), wait_send)
+    everyone = pl.ds(0, m - 1)
+    pltpu.make_async_remote_copy(
+        src_ref=total.at[everyone], dst_ref=share.at[everyone], send_sem=sent.at[2], recv_sem=floor_in.at[0],
+        device_id={"floor": lax.rem(floor + 1, m)}, device_id_type=MESH,
+    ).wait_recv()
+    result = total[floor]
+    for step in range(1, m):
+        result = result + share[lax.rem(floor + step, m)]
+    out_ref[0] = result.astype(out_ref.dtype)
+
+
+def square_call(n, m, samples, operator):
+    _, k, depth = samples.shape
+    sensors = operator.shape[1]
+    half = depth // 2
+    widths = [part * half // 16 for part in (5, 5, 4, 2)]
+    chunks = len(widths)
+    dma = pltpu.SemaphoreType.DMA
+    return pl.pallas_call(
+        functools.partial(square, m, widths, 1),
+        out_shape=pltpu.VMEM((1, k, sensors // m), jnp.bfloat16),
+        in_specs=[pl.BlockSpec(memory_space=pl.ANY)] * 2,
+        out_specs=pl.BlockSpec(memory_space=pltpu.VMEM),
+        scratch_shapes=[
+            pltpu.VMEM((n, k, half), jnp.bfloat16),
+            pltpu.VMEM((k, depth), jnp.bfloat16),
+            pltpu.VMEM((2, sensors, half), jnp.bfloat16),
+            pltpu.VMEM((n, k, 2 * sensors), jnp.float32),
+            pltpu.VMEM((n, m, k, sensors // m), jnp.float32),
+            pltpu.VMEM((n, m, k, sensors // m), jnp.float32),
+            pltpu.VMEM((m, k, sensors // m), jnp.float32),
+            pltpu.VMEM((m, k, sensors // m), jnp.float32),
+            dma((3,)), dma((2,)), dma((1,)), dma((4, chunks)), dma((3,)), dma((m,)), dma((1,)),
+            pltpu.SemaphoreType.REGULAR((3,)),
+        ],
+        compiler_params=pltpu.CompilerParams(collective_id=0, has_side_effects=True),
+    )(samples, operator)
+
+
 def solution(mesh):
     n, m = mesh.shape["tm"], mesh.shape["floor"]
 
     def local(samples, operator):
+        if grid_of(n // 2) == (2, 2):
+            return square_call(n, m, samples, operator)
         _, k, depth = samples.shape
         sensors = operator.shape[1]
         chunks = 4
         width = depth // chunks
         return pl.pallas_call(
             functools.partial(kernel, n, m, chunks),
-            out_shape=jax.ShapeDtypeStruct((1, k, sensors // m), jnp.bfloat16),
+            out_shape=pltpu.VMEM((1, k, sensors // m), jnp.bfloat16),
             in_specs=[pl.BlockSpec(memory_space=pl.ANY)] * 2,
             out_specs=pl.BlockSpec(memory_space=pltpu.VMEM),
             scratch_shapes=[

time: 28.2 us -> 23.2 us (0.82)
  the two profiles are of different devices: /device:TPU:6 before, /device:TPU:4 now
where the time goes in v3:
time: 23.2 us; the launch traced here: 23.1 us
  Pallas kernels  22.5 us (97%)
  local copies, waits for them, and re-layouts  0.6 us (3%)
    pallas_call x1, Pallas kernels, square_call(): pl.pallas_call(functools.partial(square, m, widths, 1), out_shape=pltpu.V...  22.5 us
    unnamed x1, local copies, waits for them, and re-layouts  0.6 us

profile of v3, /device:TPU:4, one launch (start us, length us, event | category | flops | bytes accessed | tf_op | source)
XLA Modules:
  0.0 23.1 jit_solution(4104920492591229211)
XLA Ops:
  0.0 22.5 %shard_map.28 = bf16[1,16,128]{2,1,0:T(8,128)(2,1)S(1)} custom-call(bf16[1,16,8192]{2,1,0:T(8,128)(2,1)} %x_hbm.1, bf16[1,512,8192]{2,1,0:T(8,128)(2,1)} %op_hbm.1), custom_call_target="tpu_custom_call" | custom-call | tf_op jit(solution)/shard_map/pallas_call | solution.py:702
  22.5 0.6 %copy.4 = bf16[1,16,128]{2,1,0:T(8,128)(2,1)} copy(bf16[1,16,128]{2,1,0:T(8,128)(2,1)S(1)} %shard_map.28) | data formatting | bytes 8192

commit v4 on v3

--- a/solution.py
+++ b/solution.py
@@ -466,12 +466,14 @@
 
     lead = chunks // 2
     staged.wait()
-    for j in range(lead):
-        @pl.when(needs_at_x)
+    for j in range(chunks):
+        at_once = jnp.logical_not(inner) | (j < lead)
+
+        @pl.when(at_once & needs_at_x)
         def _(j=j):
             send_x(j, start)
 
-        @pl.when(needs_at_y)
+        @pl.when(at_once & needs_at_y)
         def _(j=j):
             send_y(j, start)
 
@@ -525,23 +527,16 @@
     def arrive(j):
         from_x(j, needs[1], True, start)
         from_y(j, needs[2], True, start)
-        if j == split - 1:
-            @pl.when(jnp.logical_not(inner))
-            def _():
-                for late in range(lead, chunks):
-                    send_late(late)
-
     first = chip == 0
 
-    def ready(j, step):
-        if step == 0:
+    def ready(j):
+        if j == 0:
             own.wait()
             weights.wait()
             remote(x.at[other], x.at[other], sent.at[0], pair_in.at[0], pair).wait_recv()
             swapped(0)
-        if step == 2:
+        if j == 2:
             swapped(1)
-        taken(3, j, 2)
 
     def multiply(j, pieces):
         rows = jnp.concatenate([x[p, :, at(j)] for p in pieces], axis=0)
@@ -551,20 +546,17 @@
             preferred_element_type=jnp.float32,
         ).reshape(-1, k, 2 * sensors)
 
-    def compute(j, begin=False):
-        image = multiply(j, [slice(None)])
+    def compute(j, low, high, begin):
+        image = multiply(j, [slice(low, high)])
         if begin:
-            acc[...] = image
+            acc[low:high] = image
         else:
-            acc[...] += image
-
-    def compute_far(j):
+            acc[low:high] += image
+
+    def compute_ends(j):
         image = multiply(j, [slice(0, 2), slice(6, 8)])
         acc[0:2] += image[0:2]
         acc[6:8] += image[2:4]
-
-    def compute_near(j):
-        acc[2:6] += multiply(j, [slice(2, 6)])
 
     def slot_of(block):
         source = block // 2
@@ -580,16 +572,16 @@
             device_id={"tm": jnp.minimum(2 * chip + u, n - 1)}, device_id_type=MESH,
         ))
 
-    def records(places, act, add):
+    def records(places, act, add, here=True):
         def one(i, _):
             j = place(i)
-            here = pl.ds(pl.multiple_of(j * share_size, share_size), share_size)
+            mine_at = pl.ds(pl.multiple_of(j * share_size, share_size), share_size)
             there = pl.ds(pl.multiple_of(sensors + j * share_size, share_size), share_size)
             for u in places:
-                @pl.when(2 * chip + u < n)
+                @pl.when((2 * chip + u < n) & here)
                 def _(u=u):
                     if add:
-                        value = acc[slot_of(u), :, here]
+                        value = acc[slot_of(u), :, mine_at]
                         if u > 0:
                             value = value + acc[slot_of(u - 1), :, there]
                         sums[u, j] = value
@@ -604,40 +596,50 @@
 
         lax.fori_loop(0, m, one, 0)
 
-    arrive(0)
-    arrive(1)
-    swapped_order = jnp.where(inner, 1, 0)
-    for step in range(chunks - 1):
-        if step > 0:
-            @pl.when(jnp.logical_not(first))
-            def _(step=step):
-                arrive(step + 1)
-
-            if step > 1:
-                @pl.when(first)
-                def _(step=step):
-                    arrive(step)
-
-        j = (swapped_order, 1 - swapped_order)[step] if step < 2 else step
-        ready(j, step)
-        compute(j, step == 0)
-
-    ready(chunks - 1, chunks - 1)
-    pl.semaphore_wait(hello.at[1], greeted)
-
-    @pl.when(first)
+    final = chunks - 1
+
+    @pl.when(jnp.logical_not(inner))
     def _():
-        compute_far(chunks - 1)
-        records((7, 1, 0), start, True)
-        arrive(chunks - 1)
-        compute_near(chunks - 1)
-        records((6, 5, 3, 4, 2), start, True)
-
-    @pl.when(jnp.logical_not(first))
+        arrive(0)
+        arrive(1)
+        for j in range(final):
+            if j > 1:
+                arrive(j)
+            ready(j)
+            taken(3, j, 2)
+            compute(j, 0, n, j == 0)
+        ready(final)
+        taken(3, final, 2)
+        pl.semaphore_wait(hello.at[1], greeted)
+
+        @pl.when(first)
+        def _():
+            compute_ends(final)
+            records((n - 1,), start, True)
+            arrive(final)
+            compute(final, 2, 6, False)
+            records((6, 5, 3, 4, 2), start, True)
+
+        @pl.when(jnp.logical_not(first))
+        def _():
+            compute(final, 0, n, False)
+
+        records((1, 0), start, True)
+
+    @pl.when(inner)
     def _():
-        compute(chunks - 1)
-        records(range(n - 1, -1, -1), start, True)
-
+        for j in range(chunks):
+            arrive(j)
+            ready(j)
+            compute(j, 0, 6, j == 0)
+        pl.semaphore_wait(hello.at[1], greeted)
+        records((3, 2), start, True, chip == 1)
+        records((1, 0), start, True)
+        for j in [*range(split, chunks), *range(split)]:
+            taken(3, j, 2)
+            compute(j, 6, 8, j == split)
+        records((3, 2), start, True, chip == 2)
+        records((5, 4), start, True)
 
     for j in range(chunks):
         send_x(j, wait_send)
@@ -696,7 +698,7 @@
     _, k, depth = samples.shape
     sensors = operator.shape[1]
     half = depth // 2
-    widths = [part * half // 16 for part in (5, 5, 4, 2)]
+    widths = [part * half // 16 for part in (6, 6, 2, 2)]
     chunks = len(widths)
     dma = pltpu.SemaphoreType.DMA
     return pl.pallas_call(

time: 23.2 us -> 21.8 us (0.940)
  the two profiles are of different devices: /device:TPU:4 before, /device:TPU:2 now
where the time goes in v4:
time: 21.8 us; the launch traced here: 21.6 us
  Pallas kernels  21 us (96%)
  local copies, waits for them, and re-layouts  0.6 us (3%)
    pallas_call x1, Pallas kernels, square_call(): pl.pallas_call(functools.partial(square, m, widths, 1), out_shape=pltpu.V...  21 us
    unnamed x1, local copies, waits for them, and re-layouts  0.6 us

profile of v4, /device:TPU:2, one launch (start us, length us, event | category | flops | bytes accessed | tf_op | source)
XLA Modules:
  0.0 21.6 jit_solution(842292143942865595)
XLA Ops:
  0.0 21.0 %shard_map.28 = bf16[1,16,128]{2,1,0:T(8,128)(2,1)S(1)} custom-call(bf16[1,16,8192]{2,1,0:T(8,128)(2,1)} %x_hbm.1, bf16[1,512,8192]{2,1,0:T(8,128)(2,1)} %op_hbm.1), custom_call_target="tpu_custom_call" | custom-call | tf_op jit(solution)/shard_map/pallas_call | solution.py:704
  21.0 0.6 %copy.4 = bf16[1,16,128]{2,1,0:T(8,128)(2,1)} copy(bf16[1,16,128]{2,1,0:T(8,128)(2,1)S(1)} %shard_map.28) | data formatting | bytes 8192

commit v5 on v4

--- a/solution.py
+++ b/solution.py
@@ -347,7 +347,17 @@
 
     neighbours = (2 * sources[1], 2 * sources[1] + 1, 2 * sources[2], 2 * sources[2] + 1)
 
-    def greet(sem, all_round):
+    def to_upper(sem):
+        @pl.when(floor < m - 1)
+        def _():
+            pl.semaphore_signal(sem, inc=1, device_id={"floor": jnp.minimum(floor + 1, m - 1)}, device_id_type=MESH)
+
+    def to_lower(sem):
+        @pl.when(floor > 0)
+        def _():
+            pl.semaphore_signal(sem, inc=1, device_id={"floor": jnp.maximum(floor - 1, 0)}, device_id_type=MESH)
+
+    def in_plane(sem, all_round):
         pl.semaphore_signal(sem, inc=1, device_id={"tm": pair}, device_id_type=MESH)
 
         @pl.when(all_round)
@@ -355,25 +365,25 @@
             for target in neighbours:
                 pl.semaphore_signal(sem, inc=1, device_id={"tm": target}, device_id_type=MESH)
 
-        @pl.when(floor > 0)
-        def _():
-            pl.semaphore_signal(sem, inc=1, device_id={"floor": floor - 1}, device_id_type=MESH)
-
-        @pl.when(floor < m - 1)
-        def _():
-            pl.semaphore_signal(sem, inc=1, device_id={"floor": floor + 1}, device_id_type=MESH)
-
-    beside = jnp.where(floor > 0, 1, 0) + jnp.where(floor < m - 1, 1, 0)
-    greeted = 5 + beside
+    def greet(sem):
+        in_plane(sem, True)
+        to_upper(sem)
+        to_lower(sem)
+
+    below, above = jnp.where(floor > 0, 1, 0), jnp.where(floor < m - 1, 1, 0)
+    greeted = 5 + below + above
     barrier = pltpu.get_barrier_semaphore()
-    greet(barrier, chip < chips - 1)
-    pl.semaphore_wait(barrier, jnp.where(inner, 3, 5) + beside)
+    in_plane(barrier, chip < chips - 1)
+    to_upper(barrier)
+    pl.semaphore_wait(barrier, jnp.where(inner, 3, 5) + below)
 
     @pl.when(chip == chips - 1)
     def _():
         for target in neighbours:
             pl.semaphore_signal(hello.at[2], inc=1, device_id={"tm": target}, device_id_type=MESH)
 
+    to_lower(hello.at[3])
+
     def need(source, at):
         return source + at < chips
 
@@ -399,13 +409,13 @@
         @pl.when(needs_at_x | by_x(chip, core, j))
         def _():
             for half in (0, 1):
-                act(remote(mine.at[:, columns(half, j)], x.at[2 + core, :, at(j)], sent.at[0], in_sem.at[1, j], 2 * sources[1] + half))
+                act(remote(mine.at[:, columns(half, j)], x.at[2 + core, :, at(j)], sent.at[0], in_sem.at[0, j], 2 * sources[1] + half))
 
     def send_y(j, act):
         @pl.when(needs_at_y | jnp.logical_not(by_x(chip, core, j)))
         def _():
             for half in (0, 1):
-                act(remote(mine.at[:, columns(half, j)], x.at[4 + core, :, at(j)], sent.at[0], in_sem.at[2, j], 2 * sources[2] + half))
+                act(remote(mine.at[:, columns(half, j)], x.at[4 + core, :, at(j)], sent.at[0], in_sem.at[1, j], 2 * sources[2] + half))
 
     needs_at_x, needs_at_y = need(chip, sources[1]), need(chip, sources[2])
 
@@ -425,13 +435,13 @@
 
     def taken(source, j, blocks):
         here = x.at[2 * source:2 * source + blocks, :, at(j)]
-        remote(here, here, sent.at[0], in_sem.at[source, j], pair).wait_recv()
+        remote(here, here, sent.at[0], in_sem.at[source - 1, j], pair).wait_recv()
 
     def pass_x(j, parity, act):
-        act(remote(x.at[2 + parity, :, at(j)], x.at[6 + parity, :, at(j)], sent.at[0], in_sem.at[3, j], 2 * sources[2] + core))
+        act(remote(x.at[2 + parity, :, at(j)], x.at[6 + parity, :, at(j)], sent.at[0], in_sem.at[2, j], 2 * sources[2] + core))
 
     def pass_y(j, parity, act):
-        act(remote(x.at[4 + parity, :, at(j)], x.at[6 + parity, :, at(j)], sent.at[0], in_sem.at[3, j], 2 * sources[1] + core))
+        act(remote(x.at[4 + parity, :, at(j)], x.at[6 + parity, :, at(j)], sent.at[0], in_sem.at[2, j], 2 * sources[1] + core))
 
     def come(source, j, both, onward):
         count = onward[0].astype(jnp.int32) + onward[1].astype(jnp.int32)
@@ -477,8 +487,10 @@
         def _(j=j):
             send_y(j, start)
 
-    def send_only_across():
-        for j in range(chunks):
+    across = [*range(lead, chunks), *range(split, lead), *range(split)]
+
+    def send_only_across(turns):
+        for j in turns:
             @pl.when(jnp.logical_not(needs_at_x))
             def _(j=j):
                 send_x(j, start)
@@ -489,7 +501,7 @@
 
     @pl.when(chip == chips - 1)
     def _():
-        send_only_across()
+        send_only_across(range(chunks))
 
     weights.start()
     send_pair(start)
@@ -499,9 +511,13 @@
     @pl.when(inner)
     def _():
         pl.semaphore_wait(hello.at[2], 2)
-        send_only_across()
-
-    greet(hello.at[0], True)
+        send_only_across(across)
+
+    @pl.when(floor < m - 1)
+    def _():
+        pl.semaphore_wait(hello.at[3], 1)
+
+    greet(hello.at[0])
 
     def send_late(j):
         @pl.when(needs_at_x)
@@ -512,17 +528,25 @@
         def _():
             send_y(j, start)
 
-    for j in range(chunks):
+    def passing(j):
         from_x(j, jnp.logical_not(needs[1]), True, start)
         from_y(j, jnp.logical_not(needs[2]), True, start)
-        for late in range(lead, chunks):
-            if j == min(2 * (late - lead) + 1, chunks - 1):
-                @pl.when(inner)
-                def _(late=late):
+
+    @pl.when(inner)
+    def _():
+        for j in range(chunks):
+            passing(j)
+            for late in range(lead, chunks):
+                if j == min(2 * (late - lead) + 1, chunks - 1):
                     send_late(late)
 
+    @pl.when(chip == chips - 1)
+    def _():
+        for j in across:
+            passing(j)
+
     pl.semaphore_wait(hello.at[0], greeted)
-    greet(hello.at[1], True)
+    greet(hello.at[1])
 
     def arrive(j):
         from_x(j, needs[1], True, start)
@@ -564,7 +588,7 @@
         return across + block % 2
 
     def place(i):
-        return jnp.where(2 * floor >= m, i, m - 1 - i)
+        return jnp.where(i == m - 1, floor, jnp.where(i < floor, i, i + 1))
 
     def record(u, j, act):
         act(pltpu.make_async_remote_copy(
@@ -572,7 +596,7 @@
             device_id={"tm": jnp.minimum(2 * chip + u, n - 1)}, device_id_type=MESH,
         ))
 
-    def records(places, act, add, here=True):
+    def records(places, act, add, here=True, low=0, high=m):
         def one(i, _):
             j = place(i)
             mine_at = pl.ds(pl.multiple_of(j * share_size, share_size), share_size)
@@ -581,20 +605,23 @@
                 @pl.when((2 * chip + u < n) & here)
                 def _(u=u):
                     if add:
-                        value = acc[slot_of(u), :, mine_at]
-                        if u > 0:
-                            value = value + acc[slot_of(u - 1), :, there]
-                        sums[u, j] = value
-                    if u > 1:
-                        record(u, j, act)
-                    else:
-                        @pl.when(core != u)
-                        def _():
-                            record(u, j, act)
+                        sums[u, j] = acc[slot_of(u), :, mine_at] + acc[slot_of(u - 1), :, there]
+                    record(u, j, act)
 
             return 0
 
-        lax.fori_loop(0, m, one, 0)
+        lax.fori_loop(low, high, one, 0)
+
+    def swap_records(act):
+        act(remote(sums.at[other], part.at[2 * chip], sent.at[1], pair_in.at[1], pair))
+
+    def own_records():
+        for j in range(m):
+            mine_at = slice(j * share_size, (j + 1) * share_size)
+            there = slice(sensors + j * share_size, sensors + (j + 1) * share_size)
+            sums[0, j] = acc[slot_of(0), :, mine_at]
+            sums[1, j] = acc[slot_of(1), :, mine_at] + acc[slot_of(0), :, there]
+        swap_records(start)
 
     final = chunks - 1
 
@@ -615,16 +642,17 @@
         @pl.when(first)
         def _():
             compute_ends(final)
-            records((n - 1,), start, True)
+            records((n - 1,), start, True, True, 0, 1)
+            own_records()
             arrive(final)
             compute(final, 2, 6, False)
-            records((6, 5, 3, 4, 2), start, True)
+            records((6, 3, 2, 5, 4), start, True, True, 0, 1)
+            records((6, 3, 2, 5, 4, n - 1), start, True, True, 1, m)
 
         @pl.when(jnp.logical_not(first))
         def _():
             compute(final, 0, n, False)
-
-        records((1, 0), start, True)
+            own_records()
 
     @pl.when(inner)
     def _():
@@ -634,10 +662,10 @@
             compute(j, 0, 6, j == 0)
         pl.semaphore_wait(hello.at[1], greeted)
         records((3, 2), start, True, chip == 1)
-        records((1, 0), start, True)
-        for j in [*range(split, chunks), *range(split)]:
+        own_records()
+        for j in across:
             taken(3, j, 2)
-            compute(j, 6, 8, j == split)
+            compute(j, 6, 8, j == across[0])
         records((3, 2), start, True, chip == 2)
         records((5, 4), start, True)
 
@@ -660,18 +688,18 @@
     def gather_share(i, _):
         j = place(i)
 
-        for c in range(chips):
+        for c in range(1, chips):
             @pl.when(chip == c)
             def _(c=c):
                 pltpu.make_async_remote_copy(
-                    src_ref=sums.at[0:2 * c + 1, j], dst_ref=part.at[0:2 * c + 1, j], send_sem=sent.at[1],
+                    src_ref=sums.at[0:2 * c, j], dst_ref=part.at[0:2 * c, j], send_sem=sent.at[1],
                     recv_sem=red_in.at[j], device_id={"tm": pair}, device_id_type=MESH,
                 ).wait_recv()
 
         def add_part(p, value):
-            return value + part[jnp.where(p == 0, pair, 2 * chip - p), j]
-
-        total[j] = lax.fori_loop(0, 2 * chip + 1, add_part, sums[core, j])
+            return value + part[p, j]
+
+        total[j] = lax.fori_loop(0, 2 * chip, add_part, sums[core, j] + part[2 * chip, j])
 
         @pl.when(j != floor)
         def _():
@@ -679,8 +707,10 @@
 
         return 0
 
+    remote(sums.at[0], part.at[2 * chip], sent.at[1], pair_in.at[1], pair).wait_recv()
     lax.fori_loop(0, m, gather_share, 0)
-    records(range(n - 1, -1, -1), wait_send, False)
+    records(range(n - 1, 1, -1), wait_send, False)
+    swap_records(wait_send)
     for step in range(1, m):
         to_floor(lax.rem(floor + step, m), wait_send)
     everyone = pl.ds(0, m - 1)
@@ -698,7 +728,7 @@
     _, k, depth = samples.shape
     sensors = operator.shape[1]
     half = depth // 2
-    widths = [part * half // 16 for part in (6, 6, 2, 2)]
+    widths = [part * half // 16 for part in (7, 5, 2, 2)]
     chunks = len(widths)
     dma = pltpu.SemaphoreType.DMA
     return pl.pallas_call(
@@ -715,8 +745,8 @@
             pltpu.VMEM((n, m, k, sensors // m), jnp.float32),
             pltpu.VMEM((m, k, sensors // m), jnp.float32),
             pltpu.VMEM((m, k, sensors // m), jnp.float32),
-            dma((3,)), dma((2,)), dma((1,)), dma((4, chunks)), dma((3,)), dma((m,)), dma((1,)),
-            pltpu.SemaphoreType.REGULAR((3,)),
+            dma((3,)), dma((2,)), dma((2,)), dma((3, chunks)), dma((3,)), dma((m,)), dma((1,)),
+            pltpu.SemaphoreType.REGULAR((4,)),
         ],
         compiler_params=pltpu.CompilerParams(collective_id=0, has_side_effects=True),
     )(samples, operator)

time: 21.8 us -> 21.6 us (level)
  no operation moved by 1% of the time
where the time goes in v5:
time: 21.6 us; the launch traced here: 21.5 us
  Pallas kernels  20.9 us (97%)
  local copies, waits for them, and re-layouts  0.6 us (3%)
    pallas_call x1, Pallas kernels, square_call(): pl.pallas_call(functools.partial(square, m, widths, 1), out_shape=pltpu.V...  20.9 us
    unnamed x1, local copies, waits for them, and re-layouts  0.6 us

profile of v5, /device:TPU:2, one launch (start us, length us, event | category | flops | bytes accessed | tf_op | source)
XLA Modules:
  0.0 21.5 jit_solution(13155439861495356193)
XLA Ops:
  0.0 20.9 %shard_map.28 = bf16[1,16,128]{2,1,0:T(8,128)(2,1)S(1)} custom-call(bf16[1,16,8192]{2,1,0:T(8,128)(2,1)} %x_hbm.1, bf16[1,512,8192]{2,1,0:T(8,128)(2,1)} %op_hbm.1), custom_call_target="tpu_custom_call" | custom-call | tf_op jit(solution)/shard_map/pallas_call | solution.py:734
  20.9 0.6 %copy.4 = bf16[1,16,128]{2,1,0:T(8,128)(2,1)} copy(bf16[1,16,128]{2,1,0:T(8,128)(2,1)S(1)} %shard_map.28) | data formatting | bytes 8192

commit v6 on v5

--- a/solution.py
+++ b/solution.py
@@ -311,7 +311,7 @@
 
 
 def square(
-    m, widths, split, x_hbm, op_hbm, out_ref, x, mine, op, acc, sums, part, total, share,
+    m, widths, through, x_hbm, op_hbm, out_ref, x, mine, op, acc, sums, part, total, share,
     load_sem, swap_in, pair_in, in_sem, sent, red_in, floor_in, hello,
 ):
     n = part.shape[0]
@@ -391,7 +391,7 @@
 
     def by_x(source, parity, j):
         outer = (source == 0) | (source == chips - 1)
-        through_first = jnp.where(source == 1, j < split, j >= split)
+        through_first = jnp.where(source == 1, j == through, j != through)
         return (outer & (parity == j % 2)) | (jnp.logical_not(outer) & through_first)
 
     def remote(src, dst, out, into, target):
@@ -487,7 +487,7 @@
         def _(j=j):
             send_y(j, start)
 
-    across = [*range(lead, chunks), *range(split, lead), *range(split)]
+    across = [*range(lead, chunks), *(j for j in range(lead) if j != through), through]
 
     def send_only_across(turns):
         for j in turns:
@@ -728,7 +728,7 @@
     _, k, depth = samples.shape
     sensors = operator.shape[1]
     half = depth // 2
-    widths = [part * half // 16 for part in (7, 5, 2, 2)]
+    widths = [part * half // 16 for part in (5, 7, 2, 2)]
     chunks = len(widths)
     dma = pltpu.SemaphoreType.DMA
     return pl.pallas_call(

time: 21.6 us -> 21.4 us (level)
    pallas_call x1, Pallas kernels: 20.9 us -> 20.7 us  [square_call(): pl.pallas_call(functools.partial(square, m, widths, 1), out_shape=pltpu.V...]
where the time goes in v6:
time: 21.4 us; the launch traced here: 21.3 us
  Pallas kernels  20.7 us (97%)
  local copies, waits for them, and re-layouts  0.6 us (3%)
    pallas_call x1, Pallas kernels, square_call(): pl.pallas_call(functools.partial(square, m, widths, 1), out_shape=pltpu.V...  20.7 us
    unnamed x1, local copies, waits for them, and re-layouts  0.6 us

profile of v6, /device:TPU:2, one launch (start us, length us, event | category | flops | bytes accessed | tf_op | source)
XLA Modules:
  0.0 21.3 jit_solution(17346206802862987224)
XLA Ops:
  0.0 20.7 %shard_map.28 = bf16[1,16,128]{2,1,0:T(8,128)(2,1)S(1)} custom-call(bf16[1,16,8192]{2,1,0:T(8,128)(2,1)} %x_hbm.1, bf16[1,512,8192]{2,1,0:T(8,128)(2,1)} %op_hbm.1), custom_call_target="tpu_custom_call" | custom-call | tf_op jit(solution)/shard_map/pallas_call | solution.py:734
  20.7 0.6 %copy.4 = bf16[1,16,128]{2,1,0:T(8,128)(2,1)} copy(bf16[1,16,128]{2,1,0:T(8,128)(2,1)S(1)} %shard_map.28) | data formatting | bytes 8192

commit v7 on v6

--- a/solution.py
+++ b/solution.py
@@ -592,7 +592,7 @@
 
     def record(u, j, act):
         act(pltpu.make_async_remote_copy(
-            src_ref=sums.at[u, j], dst_ref=part.at[me, j], send_sem=sent.at[1], recv_sem=red_in.at[j],
+            src_ref=sums.at[u, j], dst_ref=part.at[me, j], send_sem=sent.at[0], recv_sem=red_in.at[j],
             device_id={"tm": jnp.minimum(2 * chip + u, n - 1)}, device_id_type=MESH,
         ))
 
@@ -613,7 +613,7 @@
         lax.fori_loop(low, high, one, 0)
 
     def swap_records(act):
-        act(remote(sums.at[other], part.at[2 * chip], sent.at[1], pair_in.at[1], pair))
+        act(remote(sums.at[other], part.at[2 * chip], sent.at[0], pair_in.at[1], pair))
 
     def own_records():
         for j in range(m):
@@ -669,6 +669,37 @@
         records((3, 2), start, True, chip == 2)
         records((5, 4), start, True)
 
+    def to_floor(other, act):
+        act(pltpu.make_async_remote_copy(
+            src_ref=total.at[other], dst_ref=share.at[floor],
+            send_sem=sent.at[0], recv_sem=floor_in.at[0],
+            device_id={"floor": other}, device_id_type=MESH,
+        ))
+
+    def gather_share(i, _):
+        j = place(i)
+
+        for c in range(1, chips):
+            @pl.when(chip == c)
+            def _(c=c):
+                pltpu.make_async_remote_copy(
+                    src_ref=sums.at[0:2 * c, j], dst_ref=part.at[0:2 * c, j], send_sem=sent.at[0],
+                    recv_sem=red_in.at[j], device_id={"tm": pair}, device_id_type=MESH,
+                ).wait_recv()
+
+        def add_part(p, value):
+            return value + part[p, j]
+
+        total[j] = lax.fori_loop(0, 2 * chip, add_part, sums[core, j] + part[2 * chip, j])
+
+        @pl.when(j != floor)
+        def _():
+            to_floor(j, start)
+
+        return 0
+
+    remote(sums.at[0], part.at[2 * chip], sent.at[0], pair_in.at[1], pair).wait_recv()
+    lax.fori_loop(0, m, gather_share, 0)
     for j in range(chunks):
         send_x(j, wait_send)
         send_y(j, wait_send)
@@ -677,45 +708,13 @@
     send_pair(wait_send)
     for p in (0, 1):
         swap(p, wait_send)
-
-    def to_floor(other, act):
-        act(pltpu.make_async_remote_copy(
-            src_ref=total.at[other], dst_ref=share.at[floor],
-            send_sem=sent.at[2], recv_sem=floor_in.at[0],
-            device_id={"floor": other}, device_id_type=MESH,
-        ))
-
-    def gather_share(i, _):
-        j = place(i)
-
-        for c in range(1, chips):
-            @pl.when(chip == c)
-            def _(c=c):
-                pltpu.make_async_remote_copy(
-                    src_ref=sums.at[0:2 * c, j], dst_ref=part.at[0:2 * c, j], send_sem=sent.at[1],
-                    recv_sem=red_in.at[j], device_id={"tm": pair}, device_id_type=MESH,
-                ).wait_recv()
-
-        def add_part(p, value):
-            return value + part[p, j]
-
-        total[j] = lax.fori_loop(0, 2 * chip, add_part, sums[core, j] + part[2 * chip, j])
-
-        @pl.when(j != floor)
-        def _():
-            to_floor(j, start)
-
-        return 0
-
-    remote(sums.at[0], part.at[2 * chip], sent.at[1], pair_in.at[1], pair).wait_recv()
-    lax.fori_loop(0, m, gather_share, 0)
     records(range(n - 1, 1, -1), wait_send, False)
     swap_records(wait_send)
     for step in range(1, m):
         to_floor(lax.rem(floor + step, m), wait_send)
     everyone = pl.ds(0, m - 1)
     pltpu.make_async_remote_copy(
-        src_ref=total.at[everyone], dst_ref=share.at[everyone], send_sem=sent.at[2], recv_sem=floor_in.at[0],
+        src_ref=total.at[everyone], dst_ref=share.at[everyone], send_sem=sent.at[0], recv_sem=floor_in.at[0],
         device_id={"floor": lax.rem(floor + 1, m)}, device_id_type=MESH,
     ).wait_recv()
     result = total[floor]
@@ -745,7 +744,7 @@
             pltpu.VMEM((n, m, k, sensors // m), jnp.float32),
             pltpu.VMEM((m, k, sensors // m), jnp.float32),
             pltpu.VMEM((m, k, sensors // m), jnp.float32),
-            dma((3,)), dma((2,)), dma((2,)), dma((3, chunks)), dma((3,)), dma((m,)), dma((1,)),
+            dma((3,)), dma((2,)), dma((2,)), dma((3, chunks)), dma((1,)), dma((m,)), dma((1,)),
             pltpu.SemaphoreType.REGULAR((4,)),
         ],
         compiler_params=pltpu.CompilerParams(collective_id=0, has_side_effects=True),

time: 21.4 us -> 21.4 us (level)
  no operation moved by 1% of the time
where the time goes in v7:
time: 21.4 us; the launch traced here: 21.2 us
  Pallas kernels  20.6 us (96%)
  local copies, waits for them, and re-layouts  0.6 us (3%)
    pallas_call x1, Pallas kernels, square_call(): pl.pallas_call(functools.partial(square, m, widths, 1), out_shape=pltpu.V...  20.6 us
    unnamed x1, local copies, waits for them, and re-layouts  0.6 us

profile of v7, /device:TPU:2, one launch (start us, length us, event | category | flops | bytes accessed | tf_op | source)
XLA Modules:
  0.0 21.2 jit_solution(9812925081179919233)
XLA Ops:
  0.0 20.6 %shard_map.28 = bf16[1,16,128]{2,1,0:T(8,128)(2,1)S(1)} custom-call(bf16[1,16,8192]{2,1,0:T(8,128)(2,1)} %x_hbm.1, bf16[1,512,8192]{2,1,0:T(8,128)(2,1)} %op_hbm.1), custom_call_target="tpu_custom_call" | custom-call | tf_op jit(solution)/shard_map/pallas_call | solution.py:733
  20.7 0.6 %copy.4 = bf16[1,16,128]{2,1,0:T(8,128)(2,1)} copy(bf16[1,16,128]{2,1,0:T(8,128)(2,1)S(1)} %shard_map.28) | data formatting | bytes 8192
